TPU v7x, 256 devices: a whole 4x4x8 slice. The times are simulated.
256 devices in a mesh: task: 8 (over z_hi, core), row: 8 (over x, z_lo), col: 4 (over y).
Axes of the slice: x: 4, y: 4, z: 8 (z_hi: 4, z_lo: 2; z = z_hi * 2 + z_lo), core: 2. Of those that a mesh axis runs over, the one named last changes fastest.
Arguments:
- activations: bfloat16 [8, 512, 13824], P('task', 'col', 'row'), may hold values from -6 to 6
- weights: bfloat16 [8, 13824, 5120], P('task', 'row', 'col'), may hold values from -0.0625 to 0.0625
- labels: int32 [8, 512], P('task'), may hold values from 0 to 127
- prototypes: bfloat16 [8, 128, 5120], P('task', None, 'col'), may hold values from -6 to 6
Outputs:
- merged: bfloat16 [13824, 5120], P('row', 'col')
- merged_out: bfloat16 [8, 512, 5120], P('task', 'row', 'col')
All inputs are finite; a program needn't handle non-finite values.
Results may differ from a plain program's by a relative error of at most 0.02.
Values may be sent and summed in bfloat16 or wider, within the bound.
A program may use at most 128 MiB of HBM per device.

v0:
```python
import jax
import jax.numpy as jnp
from jax import lax
from jax.sharding import PartitionSpec as P


def class_targets(label_rows, protos):
    count = label_rows.shape[0]
    onehot = (
        label_rows[:, None] == lax.broadcasted_iota(jnp.int32, (count, protos.shape[0]), 1)
    ).astype(jnp.bfloat16)
    return jnp.dot(onehot, protos, preferred_element_type=jnp.float32)


def local(activations, weights, labels, prototypes):
    acts = activations[0]
    weight = weights[0]
    label_row = labels[0]
    protos = prototypes[0]
    full_acts = lax.all_gather(acts, "col", axis=0, tiled=True)
    partial_out = jnp.dot(full_acts, weight, preferred_element_type=jnp.float32)
    output = lax.psum(partial_out.astype(jnp.bfloat16), "row").astype(jnp.float32)
    grad = output - class_targets(label_row, protos)
    gsq = (grad * grad).astype(jnp.bfloat16)
    wide = full_acts.astype(jnp.float32)
    asq = (wide * wide).astype(jnp.bfloat16)
    fisher = lax.dot_general(asq, gsq, (((0,), (0,)), ((), ())), preferred_element_type=jnp.float32)
    weighted = fisher * weight.astype(jnp.float32)
    numer, denom = (
        lax.psum_scatter(weighted, "task", scatter_dimension=0, tiled=True),
        lax.psum_scatter(fisher, "task", scatter_dimension=0, tiled=True),
    )
    piece = (numer / (denom + 1e-06)).astype(jnp.bfloat16)
    merged = lax.all_gather(piece, "task", axis=0, tiled=True)
    result = lax.psum_scatter(
        jnp.dot(full_acts, merged, preferred_element_type=jnp.float32).astype(jnp.bfloat16),
        "row",
        scatter_dimension=0,
        tiled=True,
    )
    return (merged, result[None])


def solution(mesh):
    placed = (
        P("task", "col", "row"),
        P("task", "row", "col"),
        P("task", None),
        P("task", None, "col"),
    )
    return jax.shard_map(
        local,
        mesh=mesh,
        in_specs=placed,
        out_specs=(P("row", "col"), P("task", "row", "col")),
        check_vma=False,
    )
```

profile of v0, /device:TPU:8, one launch (start us, length us, event | category | flops | bytes accessed | tf_op | source)
XLA Modules:
  0.0 475.8 jit_solution(1805810077636972893)
XLA Ops:
  7.2 0.0 copy-start
  7.2 0.0 all-gather.6.cloned.1.call-start
  7.2 0.7 all-gather.6.cloned.1.call-update
  7.9 0.0 copy-start.2
  7.9 0.0 all-reduce.2.cloned.1.call-start
  8.0 38.4 %all-gather.6.cloned.1.call-done = bf16[1,512,1728]{1,2,0:T(8,128)(2,1)} async-done(((bf16[1,128,1728]{1,2,0:T(8,128)(2,1)}), bf16[1,512,1728]{1,2,0:T(8,128)(2,1)}) %all-gather.6.cloned.1.call-update) | async-done | bytes 1769488 | tf_op jit(solution)/shard_map/all_gather | solution.py:20
  46.4 0.0 copy-start.1
  46.4 6.6 %fusion.4 = bf16[512,1280]{1,0:T(8,128)(2,1)} fusion(bf16[1,1728,1280]{2,1,0:T(8,128)(2,1)} %param.5, bf16[1,512,1728]{1,2,0:T(8,128)(2,1)} %all-gather.6.cloned.1.call-done), kind=kOutput, calls=%fused_computation.7 | convolution fusion | flops 2265579520 | bytes 7503872 | tf_op jit(solution)/shard_map/dot_general | solution.py:21
  53.0 0.0 all-reduce.2.cloned.1.call-update
  53.0 0.0 reduce-scatter.6.cloned.1.call-start
  53.1 90.5 %all-reduce.2.cloned.1.call-done = bf16[512,1280]{1,0:T(8,128)(2,1)} async-done(((bf16[512,1280]{1,0:T(8,128)(2,1)}), bf16[512,1280]{1,0:T(8,128)(2,1)}) %all-reduce.2.cloned.1.call-update) | async-done | bytes 1310736 | tf_op jit(solution)/shard_map/psum | solution.py:22
  143.6 0.0 copy-done
  143.6 0.0 copy-done.2
  143.6 0.0 copy-done.1
  143.6 9.8 %convert_multiply_fusion = (f32[1728,1280]{1,0:T(8,128)}, f32[1728,1280]{1,0:T(8,128)}) fusion(bf16[1,1728,1280]{2,1,0:T(8,128)(2,1)} %param.5, bf16[512,1280]{1,0:T(8,128)(2,1)} %all-reduce.2.cloned.1.call-done, bf16[1,128,1280]{2,1,0:T(8,128)(2,1)S(1)} %copy-done, s32[512]{0:T(512)S(1)} %bitcast.30, bf16[1,512,1728]{1,2,0:T(8,128)(2,1)S(1)} %copy-done.1), kind=kOutput, calls=%fused_computation | convolution fusion | flops 2442461184 | bytes 25528320 | tf_op jit(solution)/shard_map/dot_general | solution.py:27
  153.4 0.0 reduce-scatter.6.cloned.1.call-update
  153.4 0.0 reduce-scatter.8.cloned.1.call-start
  153.4 0.5 reduce-scatter.8.cloned.1.call-update
  154.0 0.0 all-gather.4.cloned.1.call-start
  154.0 96.8 %reduce-scatter.6.cloned.1.call-done = f32[216,1280]{1,0:T(8,128)} async-done(((f32[1728,1280]{1,0:T(8,128)}), f32[216,1280]{1,0:T(8,128)}) %reduce-scatter.6.cloned.1.call-update) | async-done | bytes 1105936 | tf_op jit(solution)/shard_map/reduce_scatter | solution.py:30
  250.8 104.8 %reduce-scatter.8.cloned.1.call-done = f32[216,1280]{1,0:T(8,128)} async-done(((f32[1728,1280]{1,0:T(8,128)}), f32[216,1280]{1,0:T(8,128)}) %reduce-scatter.8.cloned.1.call-update) | async-done | bytes 1105936 | tf_op jit(solution)/shard_map/reduce_scatter | solution.py:31
  355.7 2.5 divide_convert_fusion
  358.2 0.0 all-gather.4.cloned.1.call-update
  358.2 0.0 reduce-scatter.10.cloned.1.call-start
  358.3 54.9 %all-gather.4.cloned.1.call-done = bf16[1728,1280]{1,0:T(8,128)(2,1)} async-done(((bf16[216,1280]{1,0:T(8,128)(2,1)}), bf16[1728,1280]{1,0:T(8,128)(2,1)}) %all-gather.4.cloned.1.call-update) | async-done | bytes 4423696 | tf_op jit(solution)/shard_map/all_gather | solution.py:34
  413.1 4.8 %fusion.7 = bf16[512,1280]{0,1:T(8,128)(2,1)S(1)} fusion(bf16[1728,1280]{1,0:T(8,128)(2,1)} %all-gather.4.cloned.1.call-done, bf16[1,512,1728]{1,2,0:T(8,128)(2,1)S(1)} %copy-done.1), kind=kOutput, calls=%fused_computation.9 | convolution fusion | flops 2265579520 | bytes 7503872 | tf_op jit(solution)/shard_map/dot_general | solution.py:36
  418.0 1.4 copy.8
  419.4 0.0 reduce-scatter.10.cloned.1.call-update
  419.4 42.9 %reduce-scatter.10.cloned.1.call-done = bf16[64,1280]{1,0:T(8,128)(2,1)} async-done(((bf16[512,1280]{1,0:T(8,128)(2,1)}), bf16[64,1280]{1,0:T(8,128)(2,1)}) %reduce-scatter.10.cloned.1.call-update) | async-done | bytes 163856
  462.4 1.1 copy.9
  463.5 0.8 copy.7
  464.3 4.6 copy.12
Async XLA Ops:
  7.2 136.4 %copy-start = (bf16[1,128,1280]{2,1,0:T(8,128)(2,1)S(1)}, bf16[1,128,1280]{2,1,0:T(8,128)(2,1)}, u32[]{:S(2)}) copy-start(bf16[1,128,1280]{2,1,0:T(8,128)(2,1)} %param.7) | copy-start | bytes 983044
  7.2 39.2 %all-gather.6.cloned.1.call-start = ((), (), s32[]{:S(2)}) async-start(), calls=%async_computation.7 | async-start | bytes 2211840 | tf_op jit(solution)/shard_map/all_gather | solution.py:20
  7.9 135.7 %copy-start.2 = (s32[1,512]{1,0:T(1,128)S(1)}, s32[1,512]{1,0:T(1,128)}, u32[]{:S(2)}) copy-start(s32[1,512]{1,0:T(1,128)} %param.6) | copy-start | bytes 6148
  7.9 135.7 %all-reduce.2.cloned.1.call-start = ((), (), s32[]{:S(2)}) async-start(), calls=%async_computation.3 | async-start | bytes 2621440 | tf_op jit(solution)/shard_map/psum | solution.py:22
  46.4 97.2 %copy-start.1 = (bf16[1,512,1728]{1,2,0:T(8,128)(2,1)S(1)}, bf16[1,512,1728]{1,2,0:T(8,128)(2,1)}, u32[]{:S(2)}) copy-start(bf16[1,512,1728]{1,2,0:T(8,128)(2,1)} %all-gather.6.cloned.1.call-done) | copy-start | bytes 5308420
  53.0 197.8 %reduce-scatter.6.cloned.1.call-start = ((), (), s32[]{:S(2)}) async-start(), calls=%async_computation.4 | async-start | bytes 9953280 | tf_op jit(solution)/shard_map/reduce_scatter | solution.py:30
  153.4 202.3 %reduce-scatter.8.cloned.1.call-start = ((), (), s32[]{:S(2)}) async-start(), calls=%async_computation.5 | async-start | bytes 9953280 | tf_op jit(solution)/shard_map/reduce_scatter | solution.py:31
  154.0 259.2 %all-gather.4.cloned.1.call-start = ((), (), s32[]{:S(2)}) async-start(), calls=%async_computation.6 | async-start | bytes 4976640 | tf_op jit(solution)/shard_map/all_gather | solution.py:34
  358.2 104.1 %reduce-scatter.10.cloned.1.call-start = ((), (), s32[]{:S(2)}) async-start(), calls=%async_computation.8 | async-start | bytes 1474560
Sparse Core Ops, SparseCore 0:
  9.8 36.5 all-gather.5
  53.1 90.4 all-reduce.1
  153.5 97.2 reduce-scatter.5
  253.4 102.1 reduce-scatter.7
  358.3 54.7 all-gather.3
  419.6 42.7 reduce-scatter.9
where the time goes:
time: 476 us
  waiting for transfers between devices  430 us (90%)
  matrix products  21.2 us (4%)
  between operations  14.1 us (3%)
  local copies, waits for them, and re-layouts  8.06 us (2%)
    reduce_scatter x1, waiting for transfers between devices, local(): lax.psum_scatter(fisher, 'task', scatter_dimension=0, tiled=True)  105 us
    reduce_scatter x1, waiting for transfers between devices, local(): lax.psum_scatter(weighted, 'task', scatter_dimension=0, tiled=True)  96.8 us
    psum x1, waiting for transfers between devices, local(): lax.psum(partial_out.astype(jnp.bfloat16), 'row').astype(jnp.float32)  90.5 us
    all_gather x1, waiting for transfers between devices, local(): merged = lax.all_gather(piece, 'task', axis=0, tiled=True)  54.9 us
    unnamed x7, waiting for transfers between devices  44.2 us
    all_gather x1, waiting for transfers between devices, local(): full_acts = lax.all_gather(acts, 'col', axis=0, tiled=True)  38.4 us
    dot_general x1, matrix products, local(): lax.dot_general(asq, gsq, (((0,), (0,)), ((), ())), preferred_element_typ...  9.77 us
  transfers between devices with their start and end apart: 6, of which 6 were waited for; matrix products, arithmetic and copies ran while one was open for 0% of the time, Pallas kernels for 0%

commit v1 on v0

--- a/solution.py
+++ b/solution.py
@@ -17,7 +17,12 @@
     weight = weights[0]
     label_row = labels[0]
     protos = prototypes[0]
-    full_acts = lax.all_gather(acts, "col", axis=0, tiled=True)
+    ring = [acts]
+    for hop in range(3):
+        ring.append(lax.ppermute(ring[-1], "col", [(dev, (dev + 1) % 4) for dev in range(4)]))
+    full_acts = jnp.roll(
+        jnp.concatenate(ring[::-1], axis=0), (lax.axis_index("col") + 1) * ring[0].shape[0], axis=0
+    )
     partial_out = jnp.dot(full_acts, weight, preferred_element_type=jnp.float32)
     output = lax.psum(partial_out.astype(jnp.bfloat16), "row").astype(jnp.float32)
     grad = output - class_targets(label_row, protos)

time: 476 us -> 472 us (level)
  waiting for transfers between devices: 430 us -> 421 us
  starting transfers between devices: 0.24 us -> 5.2 us
    unnamed x7 -> x5, waiting for transfers between devices: 44.2 us -> 0.75 us
    reduce_scatter x0 -> x1, waiting for transfers between devices: none -> 42.9 us  [local(): lax.psum_scatter(jnp.dot(full_acts, merged, preferred_element_type=jnp.fl...]
    all_gather x1 -> x0, waiting for transfers between devices: 38.4 us -> none  [local(): full_acts = lax.all_gather(acts, 'col', axis=0, tiled=True)]
    ppermute x0 -> x3, waiting for transfers between devices: none -> 28 us  [local(): lax.ppermute(ring[-1], 'col', [(dev, (dev + 1) % 4) for dev in range(4)])]
    ppermute x0 -> x3, starting transfers between devices: none -> 5 us  [local(): lax.ppermute(ring[-1], 'col', [(dev, (dev + 1) % 4) for dev in range(4)])]
  transfers between devices with their start and end apart: 6 -> 8, of which waited for: 6 -> 8; matrix products, arithmetic and copies ran while one was open for 0% -> 0% of each run, Pallas kernels for 0% -> 0%
where the time goes in v1:
time: 472 us
  waiting for transfers between devices  421 us (89%)
  matrix products  20.6 us (4%)
  between operations  13.9 us (3%)
  local copies, waits for them, and re-layouts  8.61 us (2%)
  starting transfers between devices  5.2 us (1%)
    reduce_scatter x1, waiting for transfers between devices, local(): lax.psum_scatter(fisher, 'task', scatter_dimension=0, tiled=True)  104 us
    reduce_scatter x1, waiting for transfers between devices, local(): lax.psum_scatter(weighted, 'task', scatter_dimension=0, tiled=True)  96.2 us
    psum x1, waiting for transfers between devices, local(): lax.psum(partial_out.astype(jnp.bfloat16), 'row').astype(jnp.float32)  92.9 us
    all_gather x1, waiting for transfers between devices, local(): merged = lax.all_gather(piece, 'task', axis=0, tiled=True)  57.2 us
    reduce_scatter x1, waiting for transfers between devices, local(): lax.psum_scatter(jnp.dot(full_acts, merged, preferred_element_type=jnp.fl...  42.9 us
    ppermute x3, waiting for transfers between devices, local(): lax.ppermute(ring[-1], 'col', [(dev, (dev + 1) % 4) for dev in range(4)])  28 us
    dot_general x1, matrix products, local(): lax.dot_general(asq, gsq, (((0,), (0,)), ((), ())), preferred_element_typ...  10.4 us
  transfers between devices with their start and end apart: 8, of which 8 were waited for; matrix products, arithmetic and copies ran while one was open for 0% of the time, Pallas kernels for 0%

profile of v1, /device:TPU:8, one launch (start us, length us, event | category | flops | bytes accessed | tf_op | source)
XLA Modules:
  0.0 472.3 jit_solution(18210717580032254319)
XLA Ops:
  7.2 0.0 all-reduce.2.cloned.1.call-start
  7.2 1.7 collective-permute-start
  8.9 10.5 %collective-permute-done = bf16[128,1728]{0,1:T(8,128)(2,1)S(1)} collective-permute-done((bf16[128,1728]{0,1:T(8,128)(2,1)}, bf16[128,1728]{0,1:T(8,128)(2,1)S(1)}, u32[]{:S(2)}, u32[]{:S(2)}) %collective-permute-start) | collective-permute-done | bytes 442400 | tf_op jit(solution)/shard_map/ppermute | solution.py:22
  19.4 1.6 collective-permute-start.1
  21.0 9.3 %collective-permute-done.1 = bf16[128,1728]{0,1:T(8,128)(2,1)S(1)} collective-permute-done((bf16[128,1728]{0,1:T(8,128)(2,1)S(1)}, bf16[128,1728]{0,1:T(8,128)(2,1)S(1)}, u32[]{:S(2)}, u32[]{:S(2)}) %collective-permute-start.1) | collective-permute-done | bytes 442400 | tf_op jit(solution)/shard_map/ppermute | solution.py:22
  30.3 1.8 collective-permute-start.2
  32.0 8.2 %collective-permute-done.2 = bf16[128,1728]{0,1:T(8,128)(2,1)S(1)} collective-permute-done((bf16[128,1728]{0,1:T(8,128)(2,1)S(1)}, bf16[128,1728]{0,1:T(8,128)(2,1)S(1)}, u32[]{:S(2)}, u32[]{:S(2)}) %collective-permute-start.2) | collective-permute-done | bytes 442400 | tf_op jit(solution)/shard_map/ppermute | solution.py:22
  40.2 0.1 constant_dynamic-update-slice_fusion.7
  40.3 0.1 constant_dynamic-update-slice_fusion.6
  40.5 0.1 constant_dynamic-update-slice_fusion.5
  40.6 1.2 constant_dynamic-update-slice_fusion.4
  41.8 0.1 constant_dynamic-update-slice_fusion.3
  42.0 0.1 constant_dynamic-update-slice_fusion.2
  42.1 0.1 constant_dynamic-update-slice_fusion.1
  42.3 0.1 constant_dynamic-update-slice_fusion
  42.5 1.8 copy-done.3
  44.2 3.8 fusion.4
  48.0 0.0 all-reduce.2.cloned.1.call-update
  48.1 0.0 reduce-scatter.4.cloned.1.call-start
  48.1 92.9 %all-reduce.2.cloned.1.call-done = bf16[512,1280]{1,0:T(8,128)(2,1)} async-done(((bf16[512,1280]{1,0:T(8,128)(2,1)}), bf16[512,1280]{1,0:T(8,128)(2,1)}) %all-reduce.2.cloned.1.call-update) | async-done | bytes 1310736 | tf_op jit(solution)/shard_map/psum | solution.py:27
  141.0 10.4 %convert_multiply_fusion = (f32[1728,1280]{1,0:T(8,128)}, f32[1728,1280]{1,0:T(8,128)}) fusion(bf16[1,1728,1280]{2,1,0:T(8,128)(2,1)} %param.5, bf16[512,1280]{1,0:T(8,128)(2,1)} %all-reduce.2.cloned.1.call-done, bf16[1,128,1280]{2,1,0:T(8,128)(2,1)S(1)} %copy-done, s32[512]{0:T(512)S(1)} %bitcast.19, bf16[1024,1728]{0,1:T(8,128)(2,1)} %copy-done.3, ...), kind=kOutput, calls=%fused_computation | convolution fusion | flops 2442461184 | bytes 25528324 | tf_op jit(solution)/shard_map/dot_general | solution.py:32
  151.4 0.0 reduce-scatter.6.cloned.1.call-start
  151.5 0.7 reduce-scatter.6.cloned.1.call-update
  152.2 0.0 all-gather.2.cloned.1.call-start
  152.2 96.2 %reduce-scatter.4.cloned.1.call-done = f32[216,1280]{1,0:T(8,128)} async-done(((f32[1728,1280]{1,0:T(8,128)}), f32[216,1280]{1,0:T(8,128)}) %reduce-scatter.4.cloned.1.call-update) | async-done | bytes 1105936 | tf_op jit(solution)/shard_map/reduce_scatter | solution.py:35
  248.4 103.5 %reduce-scatter.6.cloned.1.call-done = f32[216,1280]{1,0:T(8,128)} async-done(((f32[1728,1280]{1,0:T(8,128)}), f32[216,1280]{1,0:T(8,128)}) %reduce-scatter.6.cloned.1.call-update) | async-done | bytes 1105936 | tf_op jit(solution)/shard_map/reduce_scatter | solution.py:36
  351.9 2.6 divide_convert_fusion
  354.4 0.0 reduce-scatter.8.cloned.1.call-start
  354.5 57.2 %all-gather.2.cloned.1.call-done = bf16[1728,1280]{1,0:T(8,128)(2,1)} async-done(((bf16[216,1280]{1,0:T(8,128)(2,1)}), bf16[1728,1280]{1,0:T(8,128)(2,1)}) %all-gather.2.cloned.1.call-update) | async-done | bytes 4423696 | tf_op jit(solution)/shard_map/all_gather | solution.py:39
  411.7 6.5 %convolution_convert_fusion = bf16[512,1280]{1,0:T(8,128)(2,1)} fusion(bf16[1728,1280]{1,0:T(8,128)(2,1)} %all-gather.2.cloned.1.call-done, bf16[1024,1728]{0,1:T(8,128)(2,1)} %copy-done.3, s32[]{:T(128)S(6)} %select_n.14), kind=kOutput, calls=%fused_computation.8 | convolution fusion | flops 2265579520 | bytes 7503876 | tf_op jit(solution)/shard_map/dot_general | solution.py:41
  418.2 42.9 %reduce-scatter.8.cloned.1.call-done = bf16[64,1280]{1,0:T(8,128)(2,1)} async-done(((bf16[512,1280]{1,0:T(8,128)(2,1)}), bf16[64,1280]{1,0:T(8,128)(2,1)}) %reduce-scatter.8.cloned.1.call-update) | async-done | bytes 163856 | tf_op jit(solution)/shard_map/reduce_scatter | solution.py:40
  461.1 4.6 copy.15
  (12 shorter events, 0.1 us)
Async XLA Ops:
  7.2 133.9 %copy-start = (bf16[1,128,1280]{2,1,0:T(8,128)(2,1)S(1)}, bf16[1,128,1280]{2,1,0:T(8,128)(2,1)}, u32[]{:S(2)}) copy-start(bf16[1,128,1280]{2,1,0:T(8,128)(2,1)} %param.7) | copy-start | bytes 983044
  7.2 35.1 %copy-start.2 = (bf16[1,128,1728]{1,2,0:T(8,128)(2,1)S(1)}, bf16[1,128,1728]{1,2,0:T(8,128)(2,1)}, u32[]{:S(2)}) copy-start(bf16[1,128,1728]{1,2,0:T(8,128)(2,1)} %param.4) | copy-start | bytes 1327108
  7.2 133.8 %all-reduce.2.cloned.1.call-start = ((), (), s32[]{:S(2)}) async-start(), calls=%async_computation.3 | async-start | bytes 2621440 | tf_op jit(solution)/shard_map/psum | solution.py:27
  7.2 12.2 %collective-permute-start = (bf16[128,1728]{0,1:T(8,128)(2,1)}, bf16[128,1728]{0,1:T(8,128)(2,1)S(1)}, u32[]{:S(2)}, u32[]{:S(2)}) collective-permute-start(bf16[128,1728]{0,1:T(8,128)(2,1)} %bitcast.18), channel_id=1, source_target_pairs={{0,1},{1,2},{2,3},{3,0},{4,5},{5,6},{6,7},{7,4},{8,9},{9,10},{10,1... | collective-permute-start | bytes 1327112 | tf_op jit(solution)/shard_map/ppermute | solution.py:22
  19.4 10.8 %collective-permute-start.1 = (bf16[128,1728]{0,1:T(8,128)(2,1)S(1)}, bf16[128,1728]{0,1:T(8,128)(2,1)S(1)}, u32[]{:S(2)}, u32[]{:S(2)}) collective-permute-start(bf16[128,1728]{0,1:T(8,128)(2,1)S(1)} %collective-permute-done), channel_id=1, source_target_pairs={{0,1},{1,2},{2,3},{3,0},{4,5},{5,6},{6,7},{7,4},{8,9},{9,10},{10,1... | collective-permute-start | bytes 1327112 | tf_op jit(solution)/shard_map/ppermute | solution.py:22
  30.3 9.9 %collective-permute-start.2 = (bf16[128,1728]{0,1:T(8,128)(2,1)S(1)}, bf16[128,1728]{0,1:T(8,128)(2,1)S(1)}, u32[]{:S(2)}, u32[]{:S(2)}) collective-permute-start(bf16[128,1728]{0,1:T(8,128)(2,1)S(1)} %collective-permute-done.1), channel_id=1, source_target_pairs={{0,1},{1,2},{2,3},{3,0},{4,5},{5,6},{6,7},{7,4},{8,9},{9,10},{10,1... | collective-permute-start | bytes 1327112 | tf_op jit(solution)/shard_map/ppermute | solution.py:22
  32.0 12.2 %copy-start.1 = (bf16[1,1728,1280]{2,1,0:T(8,128)(2,1)S(1)}, bf16[1,1728,1280]{2,1,0:T(8,128)(2,1)}, u32[]{:S(2)}) copy-start(bf16[1,1728,1280]{2,1,0:T(8,128)(2,1)} %param.5) | copy-start | bytes 13271044
  42.4 1.8 copy-start.3
  44.2 96.8 %copy-start.4 = (s32[1,512]{1,0:T(1,128)S(1)}, s32[1,512]{1,0:T(1,128)}, u32[]{:S(2)}) copy-start(s32[1,512]{1,0:T(1,128)} %param.6) | copy-start | bytes 6148
  48.1 200.3 %reduce-scatter.4.cloned.1.call-start = ((), (), s32[]{:S(2)}) async-start(), calls=%async_computation.4 | async-start | bytes 9953280 | tf_op jit(solution)/shard_map/reduce_scatter | solution.py:35
  151.4 200.4 %reduce-scatter.6.cloned.1.call-start = ((), (), s32[]{:S(2)}) async-start(), calls=%async_computation.5 | async-start | bytes 9953280 | tf_op jit(solution)/shard_map/reduce_scatter | solution.py:36
  152.2 259.5 %all-gather.2.cloned.1.call-start = ((), (), s32[]{:S(2)}) async-start(), calls=%async_computation.6 | async-start | bytes 4976640 | tf_op jit(solution)/shard_map/all_gather | solution.py:39
  354.4 106.7 %reduce-scatter.8.cloned.1.call-start = ((), (), s32[]{:S(2)}) async-start(), calls=%async_computation.7 | async-start | bytes 1474560 | tf_op jit(solution)/shard_map/reduce_scatter | solution.py:40
Sparse Core Ops, SparseCore 0:
  48.2 92.8 all-reduce.1
  151.5 96.7 reduce-scatter.3
  251.1 100.6 reduce-scatter.5
  354.6 57.0 all-gather.1
  418.3 42.7 reduce-scatter.7
